TPU v7x, 256 devices: a whole 4x4x8 slice. The times are simulated.
256 devices in a mesh: seq: 32 (over x, z), ch: 8 (over y, core).
Axes of the slice: x: 4, y: 4, z: 8, core: 2. Of those that a mesh axis runs over, the one named last changes fastest.
Arguments:
- out_gate: bfloat16 [12288, 4096], P('seq', 'ch'), may hold values from -6 to 6
- in_gate: bfloat16 [12288, 4096], P('seq', 'ch'), may hold values from -6 to 6
- values: bfloat16 [12288, 4096], P('seq', 'ch'), may hold values from -6 to 6
- short_filter: float32 [3, 3, 4096], P(None, None, 'ch'), may hold values from -3 to 3
- long_filter: float32 [12288, 4096], P('seq', 'ch'), may hold values from -1.5 to 1.5
- skip_gain: float32 [4096], P('ch'), may hold values from -4 to 4
- out_weight: bfloat16 [4096, 4096], P(None, 'ch'), may hold values from -0.09375 to 0.09375
Outputs:
- projected: bfloat16 [12288, 4096], P('seq', 'ch')
All inputs are finite; a program needn't handle non-finite values.
Results may differ from a plain program's by a relative error of at most 0.0049.
Values may be sent and summed in bfloat16 or wider, within the bound.
A program may use at most 128 MiB of HBM per device.

v0:
```python
import math
import jax
import jax.numpy as jnp
import numpy as np
from jax import lax
from jax.sharding import PartitionSpec as P

high = lax.Precision.HIGH


def contract(pattern, first_op, second_op):
    return jnp.einsum(
        pattern, first_op, second_op, precision=high, preferred_element_type=jnp.float32
    )


def tables(seq_len, inner):
    total = 2 * seq_len
    outer = total // inner
    half = seq_len // inner
    k1 = np.arange(outer)[:, None]
    n1 = np.arange(half)[None, :]
    a1 = 2.0 * np.pi * (k1 * n1 % outer) / outer
    n2 = np.arange(inner)[None, :]
    at = 2.0 * np.pi * (k1 * n2 % total) / total
    m2 = np.arange(inner)
    a2 = 2.0 * np.pi * (m2[:, None] * m2[None, :] % inner) / inner
    f32 = lambda v: jnp.asarray(v, jnp.float32)
    return dict(
        c1=f32(np.cos(a1)),
        s1=f32(np.sin(a1)),
        tc=f32(np.cos(at)[:, :, None]),
        ts=f32(np.sin(at)[:, :, None]),
        c2=f32(np.cos(a2)),
        s2=f32(np.sin(a2)),
        c1i=f32(np.cos(a1).T / total),
        s1i=f32(np.sin(a1).T / total),
    )


def forward(signal, tb):
    br = contract("kn,nmc->kmc", tb["c1"], signal)
    bi = -contract("kn,nmc->kmc", tb["s1"], signal)
    tr, ti = (tb["tc"], -tb["ts"])
    br, bi = (br * tr - bi * ti, br * ti + bi * tr)
    xr = contract("kmc,mj->kjc", br, tb["c2"]) + contract("kmc,mj->kjc", bi, tb["s2"])
    xi = contract("kmc,mj->kjc", bi, tb["c2"]) - contract("kmc,mj->kjc", br, tb["s2"])
    return (xr, xi)


def inverse(yr, yi, tb):
    zr = contract("kjc,jm->kmc", yr, tb["c2"]) - contract("kjc,jm->kmc", yi, tb["s2"])
    zi = contract("kjc,jm->kmc", yr, tb["s2"]) + contract("kjc,jm->kmc", yi, tb["c2"])
    tc, ts = (tb["tc"], tb["ts"])
    zr, zi = (zr * tc - zi * ts, zr * ts + zi * tc)
    return contract("nk,kmc->nmc", tb["c1i"], zr) - contract("nk,kmc->nmc", tb["s1i"], zi)


def long_conv(mixed_in, long_filter, inner):
    seq_len, width = mixed_in.shape
    half = seq_len // inner
    tb = tables(seq_len, inner)
    xr, xi = forward(mixed_in.reshape(half, inner, width), tb)
    hr, hi = forward(long_filter.reshape(half, inner, width), tb)
    yr = xr * hr - xi * hi
    yi = xr * hi + xi * hr
    return inverse(yr, yi, tb).reshape(seq_len, width)


def short_conv(signal, taps):
    tap_count = taps.shape[0]
    widened = jnp.pad(signal, ((tap_count - 1, 0), (0, 0)))
    seq_len = signal.shape[0]
    summed = taps[0] * widened[tap_count - 1 :]
    for offset in range(1, tap_count):
        start = tap_count - 1 - offset
        summed = summed + taps[offset] * widened[start : start + seq_len]
    return summed


def on_device(out_gate, in_gate, values, short_filter, long_filter, skip_gain, out_weight):
    seq_count = lax.axis_size("seq")
    seq_index = lax.axis_index("seq")
    width = out_gate.shape[1] // seq_count
    stacked = jnp.stack([out_gate, in_gate, values])
    spread = lax.all_to_all(stacked, "seq", split_axis=2, concat_axis=1, tiled=True)
    filt = lax.all_to_all(long_filter, "seq", split_axis=1, concat_axis=0, tiled=True)
    start = seq_index * width
    taps = lax.dynamic_slice_in_dim(short_filter, start, width, axis=2)
    gain = lax.dynamic_slice_in_dim(skip_gain, start, width, axis=0)
    spread = spread.astype(jnp.float32)
    gate_late = short_conv(spread[0], taps[0])
    mixed_in = short_conv(spread[1], taps[1]) * short_conv(spread[2], taps[2])
    long_out = long_conv(mixed_in, filt, 192)
    filtered = long_out + gain * mixed_in
    mixed = (gate_late * filtered).astype(jnp.bfloat16)
    mixed = lax.all_to_all(mixed, "seq", split_axis=0, concat_axis=1, tiled=True)
    summed = jnp.dot(
        lax.all_gather(mixed, "ch", axis=1, tiled=True),
        out_weight,
        preferred_element_type=jnp.float32,
    )
    return summed.astype(jnp.bfloat16)


def solution(mesh):
    return jax.shard_map(
        on_device,
        mesh=mesh,
        in_specs=(
            P("seq", "ch"),
            P("seq", "ch"),
            P("seq", "ch"),
            P(None, None, "ch"),
            P("seq", "ch"),
            P("ch"),
            P(None, "ch"),
        ),
        out_specs=P("seq", "ch"),
        check_vma=False,
    )
```

profile of v0, /device:TPU:1, one launch (start us, length us, event | category | flops | bytes accessed | tf_op | source)
XLA Modules:
  0.0 170.3 jit_solution(440597330835324851)
XLA Ops:
  6.5 2.4 %copy.57 = f32[384,512]{0,1:T(8,128)} copy(f32[384,512]{1,0:T(8,128)} %param.19) | data formatting | bytes 1572864 | tf_op args[4]
  8.9 11.9 %all-to-all-start.1 = ((f32[384,32,16]{0,2,1:T(8,128)}), f32[384,32,16]{0,2,1:T(8,128)S(1)}, u32[]{:S(2)}, u32[]{:S(2)}) async-start(f32[384,32,16]{0,2,1:T(8,128)} %bitcast.20), calls=%async_computation.1 | async-start | bytes 1572864 | tf_op jit(solution)/shard_map/all_to_all | solution.py:87
  21.0 2.3 %copy.50 = bf16[3,384,512]{1,0,2:T(4,128)(2,1)} copy(bf16[3,384,512]{2,1,0:T(8,128)(2,1)S(1)} %pad_maximum_fusion) | data formatting | bytes 2359296 | tf_op jit(solution)/shard_map/stack | solution.py:85
  23.3 16.8 %all-to-all-done.1 = f32[384,32,16]{0,2,1:T(8,128)S(1)} async-done(((f32[384,32,16]{0,2,1:T(8,128)}), f32[384,32,16]{0,2,1:T(8,128)S(1)}, u32[]{:S(2)}, u32[]{:S(2)}) %all-to-all-start.1) | async-done | bytes 786464 | tf_op jit(solution)/shard_map/all_to_all | solution.py:87
  40.1 8.4 %all-to-all-start = ((bf16[3,384,512]{1,0,2:T(4,128)(2,1)}), bf16[3,384,512]{1,0,2:T(4,128)(2,1)S(1)}, u32[]{:S(2)}, u32[]{:S(2)}) async-start(bf16[3,384,512]{1,0,2:T(4,128)(2,1)} %copy.50), calls=%async_computation | async-start | bytes 3145728 | tf_op jit(solution)/shard_map/all_to_all | solution.py:86
  50.1 1.1 copy.58
  51.3 1.4 reshape.45
  52.7 1.4 convolution_negate_fusion
  54.1 1.4 fusion.39
  57.5 2.1 %convolution_subtract_fusion = f32[128,16,192]{0,2,1:T(8,128)} fusion(f32[128,16,192]{0,2,1:T(8,128)S(1)} %fusion.23, f32[192,192,1]{0,1,2:T(8,128)S(1)} %copy-done.2, f32[128,192,16]{0,1,2:T(8,128)S(1)} %convolution_negate_fusion, f32[128,192,16]{0,1,2:T(8,128)S(1)} %fusion.39, f32[128,192]{0,1:T(8,128)S(1)} %copy-done.5, f32[128,192]{0,1:T(8,128)S(1)} %copy-done), kind=kOutput, calls=%fused_computation.28 | convolution fusion | flops 454557696 | bytes 6635520 | tf_op jit(solution)/shard_map/kmc,mj->kjc/dot_general | solution.py:12
  59.7 2.1 %convolution_add_fusion = f32[128,16,192]{0,2,1:T(8,128)} fusion(f32[128,16,192]{0,2,1:T(8,128)S(1)} %fusion.22, f32[192,192,1]{0,1,2:T(8,128)S(1)} %copy-done.2, f32[128,192,16]{0,1,2:T(8,128)S(1)} %convolution_negate_fusion, f32[128,192,16]{0,1,2:T(8,128)S(1)} %fusion.39, f32[128,192]{0,1:T(8,128)S(1)} %copy-done.5, f32[128,192]{0,1:T(8,128)S(1)} %copy-done), kind=kOutput, calls=%fused_computation.30 | convolution fusion | flops 454557696 | bytes 6635520 | tf_op jit(solution)/shard_map/kmc,mj->kjc/dot_general | solution.py:12
  61.8 23.4 %all-to-all-done = bf16[3,384,512]{1,0,2:T(4,128)(2,1)S(1)} async-done(((bf16[3,384,512]{1,0,2:T(4,128)(2,1)}), bf16[3,384,512]{1,0,2:T(4,128)(2,1)S(1)}, u32[]{:S(2)}, u32[]{:S(2)}) %all-to-all-start) | async-done | bytes 1179680 | tf_op jit(solution)/shard_map/all_to_all | solution.py:86
  87.2 1.4 convolution_negate_fusion.1
  88.7 1.4 fusion.38
  90.1 1.2 fusion.24
  94.1 1.5 multiply_subtract_fusion
  99.2 1.2 subtract_bitcast_fusion.1
  100.5 1.5 fusion.10
  102.0 1.6 subtract_bitcast_fusion
  103.6 1.7 %copy.61 = f32[64,192,16]{1,0,2:T(8,128)} copy(f32[64,192,16]{0,2,1:T(8,128)S(1)} %subtract_bitcast_fusion) | data formatting | bytes 1572864 | tf_op jit(solution)/shard_map/sub | solution.py:56
  105.4 1.7 reshape.46
  107.6 18.3 %all_to_all.44 = bf16[32,384,16]{1,2,0:T(8,128)(2,1)} all-to-all(bf16[32,384,16]{1,2,0:T(8,128)(2,1)S(1)} %bitcast.133), channel_id=1, replica_groups=mesh['seq'=32,'ch'=8] {'seq'}, dimensions={0} | all-to-all | bytes 786432 | tf_op jit(solution)/shard_map/all_to_all | solution.py:97
  126.0 31.7 %all-gather.2.cloned.1.call-done = bf16[384,4096]{0,1:T(8,128)(2,1)} async-done(((bf16[384,512]{0,1:T(8,128)(2,1)}), bf16[384,4096]{0,1:T(8,128)(2,1)}) %all-gather.2.cloned.1.call-update) | async-done | bytes 3145744 | tf_op jit(solution)/shard_map/all_gather | solution.py:99
  157.7 5.7 %convolution_convert_fusion = bf16[384,512]{1,0:T(8,128)(2,1)} fusion(bf16[384,4096]{0,1:T(8,128)(2,1)} %all-gather.2.cloned.1.call-done, bf16[4096,512]{1,0:T(8,128)(2,1)} %param.21), kind=kOutput, calls=%fused_computation.32 | convolution fusion | flops 1610809344 | bytes 7733248 | tf_op jit(solution)/shard_map/dot_general | solution.py:98
  (52 shorter events, 12.7 us)
Async XLA Ops:
  6.5 14.3 %copy-start.7 = (bf16[384,512]{1,0:T(8,128)(2,1)S(1)}, bf16[384,512]{1,0:T(8,128)(2,1)}, u32[]{:S(2)}) copy-start(bf16[384,512]{1,0:T(8,128)(2,1)} %param.17) | copy-start | bytes 1179652
  6.5 14.3 %copy-start.8 = (bf16[384,512]{1,0:T(8,128)(2,1)S(1)}, bf16[384,512]{1,0:T(8,128)(2,1)}, u32[]{:S(2)}) copy-start(bf16[384,512]{1,0:T(8,128)(2,1)} %param.16) | copy-start | bytes 1179652
  6.5 14.3 %copy-start.9 = (bf16[384,512]{1,0:T(8,128)(2,1)S(1)}, bf16[384,512]{1,0:T(8,128)(2,1)}, u32[]{:S(2)}) copy-start(bf16[384,512]{1,0:T(8,128)(2,1)} %param.15) | copy-start | bytes 1179652
  8.9 31.1 %all-to-all-start.1 = ((f32[384,32,16]{0,2,1:T(8,128)}), f32[384,32,16]{0,2,1:T(8,128)S(1)}, u32[]{:S(2)}, u32[]{:S(2)}) async-start(f32[384,32,16]{0,2,1:T(8,128)} %bitcast.20), calls=%async_computation.1 | async-start | bytes 1572864 | tf_op jit(solution)/shard_map/all_to_all | solution.py:87
  40.1 45.2 %all-to-all-start = ((bf16[3,384,512]{1,0,2:T(4,128)(2,1)}), bf16[3,384,512]{1,0,2:T(4,128)(2,1)S(1)}, u32[]{:S(2)}, u32[]{:S(2)}) async-start(bf16[3,384,512]{1,0,2:T(4,128)(2,1)} %copy.50), calls=%async_computation | async-start | bytes 3145728 | tf_op jit(solution)/shard_map/all_to_all | solution.py:86
  48.4 109.3 %all-gather.2.cloned.1.call-start = ((), (), s32[]{:S(2)}) async-start(), calls=%async_computation.3 | async-start | bytes 3538944 | tf_op jit(solution)/shard_map/all_gather | solution.py:99
  50.1 2.5 %copy-start.11 = (f32[128,64,1]{0,1,2:T(8,128)S(1)}, f32[128,64,1]{0,1,2:T(8,128)}, u32[]{:S(2)}) copy-start(f32[128,64,1]{0,1,2:T(8,128)} %constant.49) | copy-start | bytes 98308
  52.7 1.4 copy-start.10
  54.1 1.5 copy-start
  54.1 1.5 copy-start.1
  54.1 1.5 copy-start.5
  56.6 1.0 copy-start.2
  92.2 1.4 copy-start.3
  92.2 1.9 %copy-start.4 = (f32[128,16,192]{0,2,1:T(8,128)S(1)}, f32[128,16,192]{0,2,1:T(8,128)}, u32[]{:S(2)}) copy-start(f32[128,16,192]{0,2,1:T(8,128)} %convolution_add_fusion) | copy-start | bytes 4718596
  98.2 0.9 copy-start.12
  99.2 1.3 copy-start.14
  100.5 1.6 copy-start.13
  105.4 1.7 copy-start.6
Sparse Core Ops, SparseCore 0:
  126.1 31.5 all-gather.1
where the time goes:
time: 171 us; the launch traced here: 170 us
  waiting for transfers between devices  71.9 us (42%)
  matrix products  29.1 us (17%)
  starting transfers between devices  20.3 us (12%)
  blocking collectives  18.3 us (11%)
  local copies, waits for them, and re-layouts  15.1 us (9%)
  between operations  13.8 us (8%)
  other arithmetic  1.73 us (1%)
    all_gather x1, waiting for transfers between devices, on_device(): lax.all_gather(mixed, 'ch', axis=1, tiled=True)  31.7 us
    all_to_all x1, waiting for transfers between devices, on_device(): lax.all_to_all(stacked, 'seq', split_axis=2, concat_axis=1, tiled=True)  23.4 us
    dot_general x18, matrix products, contract(): jnp.einsum(pattern, first_op, second_op, precision=high, preferred_elemen...  23.4 us
    all_to_all x1, blocking collectives, on_device(): lax.all_to_all(mixed, 'seq', split_axis=0, concat_axis=1, tiled=True)  18.3 us
    all_to_all x1, waiting for transfers between devices, on_device(): lax.all_to_all(long_filter, 'seq', split_axis=1, concat_axis=0, tiled=True)  16.8 us
    all_to_all x1, starting transfers between devices, on_device(): lax.all_to_all(long_filter, 'seq', split_axis=1, concat_axis=0, tiled=True)  11.9 us
    all_to_all x1, starting transfers between devices, on_device(): lax.all_to_all(stacked, 'seq', split_axis=2, concat_axis=1, tiled=True)  8.36 us
    dot_general x1, matrix products, on_device(): jnp.dot(lax.all_gather(mixed, 'ch', axis=1, tiled=True), out_weight, pref...  5.7 us
  transfers between devices with their start and end apart: 3, of which 3 were waited for; matrix products, arithmetic and copies ran while one was open for 9% of the time, Pallas kernels for 0%

commit v1 on v0

--- a/solution.py
+++ b/solution.py
@@ -1,11 +1,41 @@
+import functools
 import math
 import jax
 import jax.numpy as jnp
 import numpy as np
 from jax import lax
 from jax.sharding import PartitionSpec as P
+from jax.lax import axis_index, axis_size, ppermute
 
 high = lax.Precision.HIGH
+
+
+def match_copies(vals, axis_id):
+    g_now, all_values, moved = (axis_size(axis_id), axis_index(axis_id), vals.shape[1])
+    leaves = []
+    for jj in range(g_now):
+        leaves.append((jj, (jj + 1) % g_now))
+    frames = []
+    for jj in range(g_now):
+        frames.append((jj, (jj - 1) % g_now))
+    arr_now = jnp.zeros((*vals.shape[:1], g_now * moved, *vals.shape[2:]), vals.dtype)
+    arr_now = lax.dynamic_update_slice_in_dim(arr_now, vals, all_values * moved, axis=1)
+    local_now = base_arr = vals
+    b_now = g_now // 2
+    for dd in range(1, b_now + 1):
+        local_now = ppermute(local_now, axis_name=axis_id, perm=leaves)
+        arr_now = lax.dynamic_update_slice_in_dim(
+            arr_now, local_now, (all_values - dd) % g_now * moved, axis=1
+        )
+        if dd < g_now - b_now:
+            base_arr = ppermute(base_arr, axis_name=axis_id, perm=frames)
+            arr_now = lax.dynamic_update_slice_in_dim(
+                arr_now, base_arr, (all_values + dd) % g_now * moved, axis=1
+            )
+    return arr_now
+
+
+step_on_the_masks = functools.partial(match_copies, axis_id="ch")
 
 
 def contract(pattern, first_op, second_op):
@@ -95,11 +125,7 @@
     filtered = long_out + gain * mixed_in
     mixed = (gate_late * filtered).astype(jnp.bfloat16)
     mixed = lax.all_to_all(mixed, "seq", split_axis=0, concat_axis=1, tiled=True)
-    summed = jnp.dot(
-        lax.all_gather(mixed, "ch", axis=1, tiled=True),
-        out_weight,
-        preferred_element_type=jnp.float32,
-    )
+    summed = jnp.dot(step_on_the_masks(mixed), out_weight, preferred_element_type=jnp.float32)
     return summed.astype(jnp.bfloat16)
 
 

time: 171 us -> 160 us (0.936)
  the two profiles are of different devices: /device:TPU:1 before, /device:TPU:32 now
where the time goes in v1:
time: 160 us; the launch traced here: 159 us
  waiting for transfers between devices  70.4 us (44%)
  matrix products  25.9 us (16%)
  starting transfers between devices  25 us (16%)
  blocking collectives  19.7 us (12%)
  local copies, waits for them, and re-layouts  16.1 us (10%)
  other arithmetic  1.73 us (1%)
    all_to_all x1, waiting for transfers between devices, on_device(): lax.all_to_all(stacked, 'seq', split_axis=2, concat_axis=1, tiled=True)  25.7 us
    ppermute x4, waiting for transfers between devices, match_copies(): local_now = ppermute(local_now, axis_name=axis_id, perm=leaves)  23.9 us
    dot_general x18, matrix products, contract(): jnp.einsum(pattern, first_op, second_op, precision=high, preferred_elemen...  23.4 us
    all_to_all x1, waiting for transfers between devices, on_device(): lax.all_to_all(long_filter, 'seq', split_axis=1, concat_axis=0, tiled=True)  20.7 us
    all_to_all x1, blocking collectives, on_device(): lax.all_to_all(mixed, 'seq', split_axis=0, concat_axis=1, tiled=True)  19.7 us
    all_to_all x1, starting transfers between devices, on_device(): lax.all_to_all(long_filter, 'seq', split_axis=1, concat_axis=0, tiled=True)  11.2 us
    ppermute x3, starting transfers between devices, match_copies(): base_arr = ppermute(base_arr, axis_name=axis_id, perm=frames)  8.87 us
    all_to_all x1, starting transfers between devices, on_device(): lax.all_to_all(stacked, 'seq', split_axis=2, concat_axis=1, tiled=True)  4.93 us
  transfers between devices with their start and end apart: 9, of which 7 were waited for; matrix products, arithmetic and copies ran while one was open for 10% of the time, Pallas kernels for 0%

profile of v1, /device:TPU:32, one launch (start us, length us, event | category | flops | bytes accessed | tf_op | source)
XLA Modules:
  0.0 159.4 jit_solution(1550677289257289783)
XLA Ops:
  0.0 2.4 %copy.57 = f32[384,512]{0,1:T(8,128)} copy(f32[384,512]{1,0:T(8,128)} %param.19) | data formatting | bytes 1572864 | tf_op args[4]
  2.4 11.2 %all-to-all-start.1 = ((f32[384,32,16]{0,2,1:T(8,128)}), f32[384,32,16]{0,2,1:T(8,128)S(1)}, u32[]{:S(2)}, u32[]{:S(2)}) async-start(f32[384,32,16]{0,2,1:T(8,128)} %bitcast.20), calls=%async_computation.1 | async-start | bytes 1572864 | tf_op jit(solution)/shard_map/all_to_all | solution.py:117
  13.8 2.3 %copy.50 = bf16[3,384,512]{1,0,2:T(4,128)(2,1)} copy(bf16[3,384,512]{2,1,0:T(8,128)(2,1)S(1)} %pad_maximum_fusion) | data formatting | bytes 2359296 | tf_op jit(solution)/shard_map/stack | solution.py:115
  16.1 20.7 %all-to-all-done.1 = f32[384,32,16]{0,2,1:T(8,128)S(1)} async-done(((f32[384,32,16]{0,2,1:T(8,128)}), f32[384,32,16]{0,2,1:T(8,128)S(1)}, u32[]{:S(2)}, u32[]{:S(2)}) %all-to-all-start.1) | async-done | bytes 786464 | tf_op jit(solution)/shard_map/all_to_all | solution.py:117
  36.8 4.9 %all-to-all-start = ((bf16[3,384,512]{1,0,2:T(4,128)(2,1)}), bf16[3,384,512]{1,0,2:T(4,128)(2,1)S(1)}, u32[]{:S(2)}, u32[]{:S(2)}) async-start(bf16[3,384,512]{1,0,2:T(4,128)(2,1)} %copy.50), calls=%async_computation | async-start | bytes 3145728 | tf_op jit(solution)/shard_map/all_to_all | solution.py:116
  45.9 1.4 convolution_negate_fusion
  50.8 2.1 %convolution_subtract_fusion = f32[128,16,192]{0,2,1:T(8,128)} fusion(f32[128,16,192]{0,2,1:T(8,128)S(1)} %fusion.23, f32[192,192,1]{0,1,2:T(8,128)S(1)} %copy-done.2, f32[128,192,16]{0,1,2:T(8,128)S(1)} %convolution_negate_fusion, f32[128,192,16]{0,1,2:T(8,128)S(1)} %fusion.39, f32[128,192]{0,1:T(8,128)S(1)} %copy-done.5, f32[128,192]{0,1:T(8,128)S(1)} %copy-done), kind=kOutput, calls=%fused_computation.28 | convolution fusion | flops 454557696 | bytes 6635520 | tf_op jit(solution)/shard_map/kmc,mj->kjc/dot_general | solution.py:42
  52.9 2.1 %convolution_add_fusion = f32[128,16,192]{0,2,1:T(8,128)} fusion(f32[128,16,192]{0,2,1:T(8,128)S(1)} %fusion.22, f32[192,192,1]{0,1,2:T(8,128)S(1)} %copy-done.2, f32[128,192,16]{0,1,2:T(8,128)S(1)} %convolution_negate_fusion, f32[128,192,16]{0,1,2:T(8,128)S(1)} %fusion.39, f32[128,192]{0,1:T(8,128)S(1)} %copy-done.5, f32[128,192]{0,1:T(8,128)S(1)} %copy-done), kind=kOutput, calls=%fused_computation.30 | convolution fusion | flops 454557696 | bytes 6635520 | tf_op jit(solution)/shard_map/kmc,mj->kjc/dot_general | solution.py:42
  55.0 25.7 %all-to-all-done = bf16[3,384,512]{1,0,2:T(4,128)(2,1)S(1)} async-done(((bf16[3,384,512]{1,0,2:T(4,128)(2,1)}), bf16[3,384,512]{1,0,2:T(4,128)(2,1)S(1)}, u32[]{:S(2)}, u32[]{:S(2)}) %all-to-all-start) | async-done | bytes 1179680 | tf_op jit(solution)/shard_map/all_to_all | solution.py:116
  82.8 1.4 convolution_negate_fusion.1
  89.7 1.5 multiply_subtract_fusion
  96.0 1.5 fusion.10
  97.5 1.6 subtract_bitcast_fusion
  99.1 1.7 %copy.61 = f32[64,192,16]{1,0,2:T(8,128)} copy(f32[64,192,16]{0,2,1:T(8,128)S(1)} %subtract_bitcast_fusion) | data formatting | bytes 1572864 | tf_op jit(solution)/shard_map/sub | solution.py:86
  100.9 1.9 %reshape.46 = f32[12288,16]{0,1:T(8,128)S(1)} reshape(f32[64,192,16]{1,0,2:T(8,128)} %copy.61) | data formatting | bytes 1572864 | tf_op jit(solution)/shard_map/reshape | solution.py:97
  103.3 19.7 %all_to_all.44 = bf16[32,384,16]{1,2,0:T(8,128)(2,1)S(1)} all-to-all(bf16[32,384,16]{1,2,0:T(8,128)(2,1)S(1)} %bitcast.132), channel_id=1, replica_groups=mesh['seq'=32,'ch'=8] {'seq'}, dimensions={0} | all-to-all | bytes 786432 | tf_op jit(solution)/shard_map/all_to_all | solution.py:127
  123.1 3.0 %collective-permute-start.1 = (bf16[384,512]{0,1:T(8,128)(2,1)S(1)}, bf16[384,512]{0,1:T(8,128)(2,1)S(1)}, u32[]{:S(2)}, u32[]{:S(2)}) collective-permute-start(bf16[384,512]{0,1:T(8,128)(2,1)S(1)} %bitcast.134), channel_id=1, source_target_pairs={{0,7},{1,0},{2,1},{3,2},{4,3},{5,4},{6,5},{7,6},{8,15},{9,8},{10,9... | collective-permute-start | bytes 1179656 | tf_op jit(solution)/shard_map/ppermute | solution.py:31
  126.0 5.5 %collective-permute-done = bf16[384,512]{0,1:T(8,128)(2,1)S(1)} collective-permute-done((bf16[384,512]{0,1:T(8,128)(2,1)S(1)}, bf16[384,512]{0,1:T(8,128)(2,1)S(1)}, u32[]{:S(2)}, u32[]{:S(2)}) %collective-permute-start) | collective-permute-done | bytes 393248 | tf_op jit(solution)/shard_map/ppermute | solution.py:26
  131.5 3.0 %collective-permute-start.3 = (bf16[384,512]{0,1:T(8,128)(2,1)S(1)}, bf16[384,512]{0,1:T(8,128)(2,1)S(1)}, u32[]{:S(2)}, u32[]{:S(2)}) collective-permute-start(bf16[384,512]{0,1:T(8,128)(2,1)S(1)} %collective-permute-done.1), channel_id=1, source_target_pairs={{0,7},{1,0},{2,1},{3,2},{4,3},{5,4},{6,5},{7,6},{8,15},{9,8},{10,9... | collective-permute-start | bytes 1179656 | tf_op jit(solution)/shard_map/ppermute | solution.py:31
  134.4 5.5 %collective-permute-done.2 = bf16[384,512]{0,1:T(8,128)(2,1)S(1)} collective-permute-done((bf16[384,512]{0,1:T(8,128)(2,1)S(1)}, bf16[384,512]{0,1:T(8,128)(2,1)S(1)}, u32[]{:S(2)}, u32[]{:S(2)}) %collective-permute-start.2) | collective-permute-done | bytes 393248 | tf_op jit(solution)/shard_map/ppermute | solution.py:26
  140.3 3.0 %collective-permute-start.5 = (bf16[384,512]{0,1:T(8,128)(2,1)S(1)}, bf16[384,512]{0,1:T(8,128)(2,1)S(1)}, u32[]{:S(2)}, u32[]{:S(2)}) collective-permute-start(bf16[384,512]{0,1:T(8,128)(2,1)S(1)} %collective-permute-done.3), channel_id=1, source_target_pairs={{0,7},{1,0},{2,1},{3,2},{4,3},{5,4},{6,5},{7,6},{8,15},{9,8},{10,9... | collective-permute-start | bytes 1179656 | tf_op jit(solution)/shard_map/ppermute | solution.py:31
  143.4 4.9 %collective-permute-done.4 = bf16[384,512]{0,1:T(8,128)(2,1)S(1)} collective-permute-done((bf16[384,512]{0,1:T(8,128)(2,1)S(1)}, bf16[384,512]{0,1:T(8,128)(2,1)S(1)}, u32[]{:S(2)}, u32[]{:S(2)}) %collective-permute-start.4) | collective-permute-done | bytes 393248 | tf_op jit(solution)/shard_map/ppermute | solution.py:26
  148.7 8.1 %collective-permute-done.6 = bf16[384,512]{0,1:T(8,128)(2,1)S(1)} collective-permute-done((bf16[384,512]{0,1:T(8,128)(2,1)S(1)}, bf16[384,512]{0,1:T(8,128)(2,1)S(1)}, u32[]{:S(2)}, u32[]{:S(2)}) %collective-permute-start.6) | collective-permute-done | bytes 393248 | tf_op jit(solution)/shard_map/ppermute | solution.py:26
  156.8 2.6 %convolution_convert_fusion = bf16[384,512]{1,0:T(8,128)(2,1)} fusion(bf16[384,4096]{0,1:T(8,128)(2,1)S(1)} %constant_dynamic-update-slice_fusion, bf16[4096,512]{1,0:T(8,128)(2,1)S(1)} %copy-done.15), kind=kOutput, calls=%fused_computation.32 | convolution fusion | flops 1610809344 | bytes 7733248 | tf_op jit(solution)/shard_map/dot_general | solution.py:128
  (74 shorter events, 21.2 us)
Async XLA Ops:
  0.0 13.6 %copy-start.7 = (bf16[384,512]{1,0:T(8,128)(2,1)S(1)}, bf16[384,512]{1,0:T(8,128)(2,1)}, u32[]{:S(2)}) copy-start(bf16[384,512]{1,0:T(8,128)(2,1)} %param.17) | copy-start | bytes 1179652
  0.0 13.6 %copy-start.8 = (bf16[384,512]{1,0:T(8,128)(2,1)S(1)}, bf16[384,512]{1,0:T(8,128)(2,1)}, u32[]{:S(2)}) copy-start(bf16[384,512]{1,0:T(8,128)(2,1)} %param.16) | copy-start | bytes 1179652
  0.0 13.6 %copy-start.9 = (bf16[384,512]{1,0:T(8,128)(2,1)S(1)}, bf16[384,512]{1,0:T(8,128)(2,1)}, u32[]{:S(2)}) copy-start(bf16[384,512]{1,0:T(8,128)(2,1)} %param.15) | copy-start | bytes 1179652
  2.4 34.4 %all-to-all-start.1 = ((f32[384,32,16]{0,2,1:T(8,128)}), f32[384,32,16]{0,2,1:T(8,128)S(1)}, u32[]{:S(2)}, u32[]{:S(2)}) async-start(f32[384,32,16]{0,2,1:T(8,128)} %bitcast.20), calls=%async_computation.1 | async-start | bytes 1572864 | tf_op jit(solution)/shard_map/all_to_all | solution.py:117
  36.8 44.0 %all-to-all-start = ((bf16[3,384,512]{1,0,2:T(4,128)(2,1)}), bf16[3,384,512]{1,0,2:T(4,128)(2,1)S(1)}, u32[]{:S(2)}, u32[]{:S(2)}) async-start(bf16[3,384,512]{1,0,2:T(4,128)(2,1)} %copy.50), calls=%async_computation | async-start | bytes 3145728 | tf_op jit(solution)/shard_map/all_to_all | solution.py:116
  43.4 2.5 %copy-start.11 = (f32[128,64,1]{0,1,2:T(8,128)S(1)}, f32[128,64,1]{0,1,2:T(8,128)}, u32[]{:S(2)}) copy-start(f32[128,64,1]{0,1,2:T(8,128)} %constant.107) | copy-start | bytes 98308
  45.9 1.4 copy-start.10
  47.4 1.5 copy-start
  47.4 1.5 copy-start.1
  47.4 1.5 copy-start.5
  49.8 1.0 copy-start.2
  87.8 1.4 copy-start.3
  87.8 1.9 %copy-start.4 = (f32[128,16,192]{0,2,1:T(8,128)S(1)}, f32[128,16,192]{0,2,1:T(8,128)}, u32[]{:S(2)}) copy-start(f32[128,16,192]{0,2,1:T(8,128)} %convolution_add_fusion) | copy-start | bytes 4718596
  94.7 1.3 copy-start.14
  96.0 1.6 copy-start.13
  100.9 1.9 %copy-start.6 = (f32[2,8,32,384]{3,1,2,0:T(8,128)S(1)}, f32[2,8,32,384]{3,1,2,0:T(8,128)}, u32[]{:S(2)}) copy-start(f32[2,8,32,384]{3,1,2,0:T(8,128)} %copy.66) | copy-start | bytes 2359300
  123.1 8.4 %collective-permute-start = (bf16[384,512]{0,1:T(8,128)(2,1)S(1)}, bf16[384,512]{0,1:T(8,128)(2,1)S(1)}, u32[]{:S(2)}, u32[]{:S(2)}) collective-permute-start(bf16[384,512]{0,1:T(8,128)(2,1)S(1)} %bitcast.133), channel_id=1, source_target_pairs={{0,1},{1,2},{2,3},{3,4},{4,5},{5,6},{6,7},{7,0},{8,9},{9,10},{10,1... | collective-permute-start | bytes 1179656 | tf_op jit(solution)/shard_map/ppermute | solution.py:26
  123.1 8.4 %collective-permute-start.1 = (bf16[384,512]{0,1:T(8,128)(2,1)S(1)}, bf16[384,512]{0,1:T(8,128)(2,1)S(1)}, u32[]{:S(2)}, u32[]{:S(2)}) collective-permute-start(bf16[384,512]{0,1:T(8,128)(2,1)S(1)} %bitcast.134), channel_id=1, source_target_pairs={{0,7},{1,0},{2,1},{3,2},{4,3},{5,4},{6,5},{7,6},{8,15},{9,8},{10,9... | collective-permute-start | bytes 1179656 | tf_op jit(solution)/shard_map/ppermute | solution.py:31
  131.5 8.4 %collective-permute-start.2 = (bf16[384,512]{0,1:T(8,128)(2,1)S(1)}, bf16[384,512]{0,1:T(8,128)(2,1)S(1)}, u32[]{:S(2)}, u32[]{:S(2)}) collective-permute-start(bf16[384,512]{0,1:T(8,128)(2,1)S(1)} %collective-permute-done), channel_id=1, source_target_pairs={{0,1},{1,2},{2,3},{3,4},{4,5},{5,6},{6,7},{7,0},{8,9},{9,10},{10,1... | collective-permute-start | bytes 1179656 | tf_op jit(solution)/shard_map/ppermute | solution.py:26
  131.5 8.8 %collective-permute-start.3 = (bf16[384,512]{0,1:T(8,128)(2,1)S(1)}, bf16[384,512]{0,1:T(8,128)(2,1)S(1)}, u32[]{:S(2)}, u32[]{:S(2)}) collective-permute-start(bf16[384,512]{0,1:T(8,128)(2,1)S(1)} %collective-permute-done.1), channel_id=1, source_target_pairs={{0,7},{1,0},{2,1},{3,2},{4,3},{5,4},{6,5},{7,6},{8,15},{9,8},{10,9... | collective-permute-start | bytes 1179656 | tf_op jit(solution)/shard_map/ppermute | solution.py:31
  139.9 8.4 %collective-permute-start.4 = (bf16[384,512]{0,1:T(8,128)(2,1)S(1)}, bf16[384,512]{0,1:T(8,128)(2,1)S(1)}, u32[]{:S(2)}, u32[]{:S(2)}) collective-permute-start(bf16[384,512]{0,1:T(8,128)(2,1)S(1)} %collective-permute-done.2), channel_id=1, source_target_pairs={{0,1},{1,2},{2,3},{3,4},{4,5},{5,6},{6,7},{7,0},{8,9},{9,10},{10,1... | collective-permute-start | bytes 1179656 | tf_op jit(solution)/shard_map/ppermute | solution.py:26
  140.3 8.3 %collective-permute-start.5 = (bf16[384,512]{0,1:T(8,128)(2,1)S(1)}, bf16[384,512]{0,1:T(8,128)(2,1)S(1)}, u32[]{:S(2)}, u32[]{:S(2)}) collective-permute-start(bf16[384,512]{0,1:T(8,128)(2,1)S(1)} %collective-permute-done.3), channel_id=1, source_target_pairs={{0,7},{1,0},{2,1},{3,2},{4,3},{5,4},{6,5},{7,6},{8,15},{9,8},{10,9... | collective-permute-start | bytes 1179656 | tf_op jit(solution)/shard_map/ppermute | solution.py:31
  143.3 13.5 %copy-start.15 = (bf16[4096,512]{1,0:T(8,128)(2,1)S(1)}, bf16[4096,512]{1,0:T(8,128)(2,1)}, u32[]{:S(2)}) copy-start(bf16[4096,512]{1,0:T(8,128)(2,1)} %param.21) | copy-start | bytes 12582916
  148.3 8.4 %collective-permute-start.6 = (bf16[384,512]{0,1:T(8,128)(2,1)S(1)}, bf16[384,512]{0,1:T(8,128)(2,1)S(1)}, u32[]{:S(2)}, u32[]{:S(2)}) collective-permute-start(bf16[384,512]{0,1:T(8,128)(2,1)S(1)} %collective-permute-done.4), channel_id=1, source_target_pairs={{0,1},{1,2},{2,3},{3,4},{4,5},{5,6},{6,7},{7,0},{8,9},{9,10},{10,1... | collective-permute-start | bytes 1179656 | tf_op jit(solution)/shard_map/ppermute | solution.py:26
  (1 other events, 0.9 us)
